TPU v7x, 32 devices: a whole 2x2x4 slice. The times are simulated.
32 devices in a mesh: lat: 4 (over y, x), lon: 8 (over z, core).
Axes of the slice: x: 2, y: 2, z: 4, core: 2. Of those that a mesh axis runs over, the one named last changes fastest.
Arguments:
- members: float32 [80, 2, 256, 1024], P('lon', None, 'lat'), may hold values from -6 to 6
- obs_row: int32 [2, 4, 8, 64], P(None, 'lat', 'lon'), may hold values from 0 to 63
- obs_col: int32 [2, 4, 8, 64], P(None, 'lat', 'lon'), may hold values from 0 to 127
- obs_value: float32 [2, 4, 8, 64], P(None, 'lat', 'lon'), may hold values from -6 to 6
- obs_error: float32 [2, 4, 8, 64], P(None, 'lat', 'lon'), may hold values from 0.25 to 4
- obs_weight: float32 [2, 4, 8, 2, 64], P(None, 'lat', 'lon'), may hold values from 0.2 to 1
- obs_count: int32 [2, 4, 8], P(None, 'lat', 'lon'), may hold values from 8 to 64, as said below
Outputs:
- analysis: float32 [80, 2, 256, 1024], P('lon', None, 'lat')
Inputs may be any that keep to these rules, and one draw needn't show every extreme that they name: The first obs_count slots of a tile hold its observations, the others are ignored; in each batch one tile holds 64. `obs_row`: row inside the owning tile. `obs_col`: column inside the owning tile.
All inputs are finite; a program needn't handle non-finite values.
Results may differ from a plain program's by a relative error of at most 0.0001.
Values sent between devices are 32-bit elements; how exact they have to be, the bound alone decides.
A program may use at most 192 MiB of HBM per device.

v0:
```python
import math
import jax
import jax.numpy as jnp
from jax import lax
from jax.sharding import PartitionSpec as P

NBATCH = 2
RAD = 48


def extended(block, sides, width):
    for axis, dim in sides:
        count = lax.axis_size(axis)
        forward = [(i, i + 1) for i in range(count - 1)]
        forward.append((count - 1, 0))
        backward = [(target, source) for source, target in forward]
        low = lax.ppermute(
            lax.slice_in_dim(block, block.shape[dim] - width, None, axis=dim), axis, forward
        )
        high = lax.ppermute(lax.slice_in_dim(block, 0, width, axis=dim), axis, backward)
        block = jnp.concatenate([low, block, high], axis=dim)
    return block


def gaspari(dist):
    z = dist / (0.5 * RAD)
    near = (((-0.25 * z + 0.5) * z + 0.625) * z - 5.0 / 3.0) * z * z + 1.0
    zfar = jnp.maximum(z, 1.0)
    far = (
        ((((zfar / 12.0 - 0.5) * zfar + 0.625) * zfar + 5.0 / 3.0) * zfar - 5.0) * zfar
        + 4.0
        - 2.0 / (3.0 * zfar)
    )
    return jnp.where(z <= 1.0, near, jnp.where(z < 2.0, far, 0.0))


def body(members, obs_row, obs_col, obs_value, obs_error, obs_weight, obs_count):
    lon_parts = lax.axis_size("lon")
    group = members.shape[0]
    full = group * lon_parts
    clat = members.shape[2]
    nlon = members.shape[3]
    clon = nlon // lon_parts
    slot_count = obs_row.shape[-1]
    lat_first = lax.axis_index("lat") * clat
    lon_first = lax.axis_index("lon") * clon
    highest = lax.Precision.HIGHEST
    state = lax.all_to_all(members, "lon", split_axis=3, concat_axis=0, tiled=True)
    first_left = 0
    for batch in range(first_left, NBATCH):
        picked = state[:, :, obs_row[batch, 0, 0], obs_col[batch, 0, 0]]
        prior = jnp.einsum("klo,lo->ko", picked, obs_weight[batch, 0, 0], precision=highest)
        valid = (jnp.arange(slot_count) < obs_count[batch, 0, 0]).astype(jnp.float32)
        prior_mean = jnp.mean(prior, axis=0)
        summarize_prior_pert = prior - prior_mean
        spread = jnp.sum(summarize_prior_pert * summarize_prior_pert, axis=0) / (full - 1.0)
        err = obs_error[batch, 0, 0]
        denom = spread + err
        summarize_mean_coef = valid * (obs_value[batch, 0, 0] - prior_mean) / denom
        summarize_pert_coef = valid / (denom * (1.0 + jnp.sqrt(err / denom)))
        glat = (lat_first + obs_row[batch, 0, 0]).astype(jnp.float32)
        glon = (lon_first + obs_col[batch, 0, 0]).astype(jnp.float32)
        extra = jnp.stack([summarize_mean_coef, summarize_pert_coef, glat, glon], axis=0)
        packed = jnp.concatenate([summarize_prior_pert, extra], axis=0)
        wide = extended(packed[:, None, None, :], (("lat", 1), ("lon", 2)), 1)
        received = wide.reshape(packed.shape[0], -1)
        members_here = state.shape[0]
        levels = state.shape[1]
        mean = jnp.mean(state, axis=0)
        pert = state - mean
        prior_pert = received[:members_here]
        mean_coef = received[members_here]
        pert_coef = received[members_here + 1]
        obs_lat = received[members_here + 2]
        obs_lon = received[members_here + 3]
        coef = mean_coef[:, None] - pert_coef[:, None] * prior_pert.T
        rows_block = math.gcd(clat, max(1, 2048 // clon))
        block_count = clat // rows_block
        cells = rows_block * clon
        blocks = jnp.moveaxis(pert.reshape(members_here, levels, block_count, cells), 2, 0)
        half = 0.5 * nlon

        def one_block(item):
            block, which = item
            local = jnp.arange(cells)
            cell_lat = (lat_first + which * rows_block + local // clon).astype(jnp.float32)
            cell_lon = (lon_first + local % clon).astype(jnp.float32)
            delta_lat = cell_lat[:, None] - obs_lat[None, :]
            delta_lon = jnp.mod(cell_lon[:, None] - obs_lon[None, :] + half, 1.0 * nlon) - half
            taper = gaspari(jnp.sqrt(delta_lat * delta_lat + delta_lon * delta_lon))
            cov = jnp.einsum("kpc,km->pcm", block, prior_pert, precision=highest) / (
                members_here - 1.0
            )
            return jnp.einsum("pcm,mk->kpc", cov * taper[None], coef, precision=highest)

        increments = lax.map(one_block, (blocks, jnp.arange(block_count)))
        state = state + jnp.moveaxis(increments, 0, 2).reshape(state.shape)
    return lax.all_to_all(state, "lon", split_axis=0, concat_axis=3, tiled=True)


def solution(mesh):
    placed = (
        P("lon", None, "lat", None),
        P(None, "lat", "lon", None),
        P(None, "lat", "lon", None),
        P(None, "lat", "lon", None),
        P(None, "lat", "lon", None),
        P(None, "lat", "lon", None, None),
        P(None, "lat", "lon"),
    )
    return jax.shard_map(
        body, mesh=mesh, in_specs=placed, out_specs=P("lon", None, "lat", None), check_vma=False
    )
```

profile of v0, /device:TPU:0, one launch (start us, length us, event | category | flops | bytes accessed | tf_op | source)
XLA Modules:
  0.0 839.3 jit_solution(459850053425190709)
XLA Ops:
  0.0 14.7 %copy.109 = f32[10,2,64,1024]{2,0,1,3:T(8,128)} copy(f32[10,2,64,1024]{3,2,1,0:T(8,128)} %param.11) | data formatting | bytes 10485760 | tf_op args[0]
  14.7 12.8 %reshape.700 = f32[8,1,163840]{2,1,0:T(1,128)} reshape(f32[1024,2,10,64]{3,2,1,0:T(8,128)} %bitcast.193) | data formatting | bytes 10485760
  35.3 115.3 %all-to-all-done = f32[8,1,163840]{2,1,0:T(1,128)} async-done(((f32[8,1,163840]{2,1,0:T(1,128)}), f32[8,1,163840]{2,1,0:T(1,128)}, u32[]{:S(2)}, u32[]{:S(2)}) %all-to-all-start) | async-done | bytes 5242912 | tf_op jit(solution)/shard_map/all_to_all | solution.py:48
  151.2 16.6 %reduce.24 = f32[8,163840]{1,0:T(8,128)} reduce(f32[8,1,163840]{2,1,0:T(1,128)} %all-to-all-done, f32[]{:T(128)} %broadcast.1090), dimensions={1}, to_apply=%all_to_all.28.reduce_sub_computation | reduce | bytes 10485764 | tf_op jit(solution)/shard_map/all_to_all | solution.py:48
  167.8 13.2 %reshape.701 = f32[1024,2,10,64]{3,2,1,0:T(8,128)} reshape(f32[8,163840]{1,0:T(8,128)} %reduce.24) | data formatting | bytes 10485760
  181.0 12.2 %copy.111 = f32[8,10,2,64,128]{4,3,2,1,0:T(8,128)} copy(f32[8,10,2,64,128]{3,1,2,4,0:T(8,128)} %bitcast.190) | data formatting | bytes 10485760 | tf_op jit(solution)/shard_map/all_to_all | solution.py:48
  193.1 8.8 %copy.113 = f32[80,2,64,128]{0,1,3,2:T(2,128)} copy(f32[80,2,64,128]{3,2,1,0:T(8,128)} %bitcast.192) | data formatting | bytes 10485760 | tf_op jit(solution)/shard_map/all_to_all | solution.py:48
  211.2 10.3 %copy.137 = f32[10,2,64,8,128]{4,3,2,1,0:T(8,128)} copy(f32[10,2,64,8,128]{2,0,1,4,3:T(8,128)} %bitcast.191) | data formatting | bytes 10485760 | tf_op jit(solution)/shard_map/all_to_all | solution.py:48
  224.3 7.3 all_to_all.32
  235.2 7.2 subtract_bitcast_fusion.1
  244.0 246.9 %while.24 = (s32[]{:T(128)}, f32[4,80,2,2048]{3,0,2,1:T(4,128)}, f32[4,80,2,2048]{3,0,2,1:T(4,128)}, f32[80,576]{1,0:T(8,128)S(1)}, s32[4]{0:T(128)S(1)}, /*inde...) while((s32[]{:T(128)}, f32[4,80,2,2048]{3,0,2,1:T(4,128)}, ...), condition=%wide.region_4.5_spmd, body=%wide.region_3.4_spmd.sunk | while | flops 4581785600 | bytes 39212736 | solution.py:96
  263.7 9.7 %fusion.114 = f32[2048,576]{0,1:T(8,128)S(1)} fusion(f32[576]{0:T(1024)S(1)} %reduce.29, f32[2048]{0:T(1024)S(1)} %get-tuple-element.559, f32[576]{0:T(1024)S(1)} %reduce.30, f32[2048]{0:T(1024)S(1)} %get-tuple-element.560), kind=kLoop, calls=%fused_computation.12.clone.1 | loop fusion | flops 49545216 | bytes 4739584 | tf_op jit(solution)/shard_map/while/body/eval_jaxpr/mul | solution.py:94
  277.2 7.8 fusion.112
  285.1 6.8 fusion.115
  293.2 24.1 %dynamic_update_slice.16 = f32[4,80,2,2048]{3,0,2,1:T(4,128)} dynamic-update-slice(f32[4,80,2,2048]{3,0,2,1:T(4,128)} %get-tuple-element.588, f32[1,80,2,2048]{3,0,2,1:T(1,128)S(1)} %copy.162, s32[]{:T(128)} %get-tuple-element.587, s32[]{:T(128)} %constant.329.clone.1..sunk, s32[]{:T(128)} %constant.329.clone.1..sunk, s32[]{:T(128)} %constant.329.clone.1..sunk) | dynamic-update-slice | bytes 2621444 | tf_op jit(solution)/shard_map/while/body/jit(dynamic_update_index_in_dim)/dynamic_update_slice | solution.py:96
  318.7 9.7 %fusion.114 = f32[2048,576]{0,1:T(8,128)S(1)} fusion(f32[576]{0:T(1024)S(1)} %reduce.29, f32[2048]{0:T(1024)S(1)} %get-tuple-element.559, f32[576]{0:T(1024)S(1)} %reduce.30, f32[2048]{0:T(1024)S(1)} %get-tuple-element.560), kind=kLoop, calls=%fused_computation.12.clone.1 | loop fusion | flops 49545216 | bytes 4739584 | tf_op jit(solution)/shard_map/while/body/eval_jaxpr/mul | solution.py:94
  332.3 7.8 fusion.112
  340.1 6.8 fusion.115
  348.3 24.1 %dynamic_update_slice.16 = f32[4,80,2,2048]{3,0,2,1:T(4,128)} dynamic-update-slice(f32[4,80,2,2048]{3,0,2,1:T(4,128)} %get-tuple-element.588, f32[1,80,2,2048]{3,0,2,1:T(1,128)S(1)} %copy.162, s32[]{:T(128)} %get-tuple-element.587, s32[]{:T(128)} %constant.329.clone.1..sunk, s32[]{:T(128)} %constant.329.clone.1..sunk, s32[]{:T(128)} %constant.329.clone.1..sunk) | dynamic-update-slice | bytes 2621444 | tf_op jit(solution)/shard_map/while/body/jit(dynamic_update_index_in_dim)/dynamic_update_slice | solution.py:96
  373.7 9.7 %fusion.114 = f32[2048,576]{0,1:T(8,128)S(1)} fusion(f32[576]{0:T(1024)S(1)} %reduce.29, f32[2048]{0:T(1024)S(1)} %get-tuple-element.559, f32[576]{0:T(1024)S(1)} %reduce.30, f32[2048]{0:T(1024)S(1)} %get-tuple-element.560), kind=kLoop, calls=%fused_computation.12.clone.1 | loop fusion | flops 49545216 | bytes 4739584 | tf_op jit(solution)/shard_map/while/body/eval_jaxpr/mul | solution.py:94
  387.3 7.8 fusion.112
  395.1 6.8 fusion.115
  403.3 24.1 %dynamic_update_slice.16 = f32[4,80,2,2048]{3,0,2,1:T(4,128)} dynamic-update-slice(f32[4,80,2,2048]{3,0,2,1:T(4,128)} %get-tuple-element.588, f32[1,80,2,2048]{3,0,2,1:T(1,128)S(1)} %copy.162, s32[]{:T(128)} %get-tuple-element.587, s32[]{:T(128)} %constant.329.clone.1..sunk, s32[]{:T(128)} %constant.329.clone.1..sunk, s32[]{:T(128)} %constant.329.clone.1..sunk) | dynamic-update-slice | bytes 2621444 | tf_op jit(solution)/shard_map/while/body/jit(dynamic_update_index_in_dim)/dynamic_update_slice | solution.py:96
  428.7 9.7 %fusion.114 = f32[2048,576]{0,1:T(8,128)S(1)} fusion(f32[576]{0:T(1024)S(1)} %reduce.29, f32[2048]{0:T(1024)S(1)} %get-tuple-element.559, f32[576]{0:T(1024)S(1)} %reduce.30, f32[2048]{0:T(1024)S(1)} %get-tuple-element.560), kind=kLoop, calls=%fused_computation.12.clone.1 | loop fusion | flops 49545216 | bytes 4739584 | tf_op jit(solution)/shard_map/while/body/eval_jaxpr/mul | solution.py:94
  442.3 7.8 fusion.112
  458.3 24.1 %dynamic_update_slice.16 = f32[4,80,2,2048]{3,0,2,1:T(4,128)} dynamic-update-slice(f32[4,80,2,2048]{3,0,2,1:T(4,128)} %get-tuple-element.588, f32[1,80,2,2048]{3,0,2,1:T(1,128)S(1)} %copy.162, s32[]{:T(128)} %get-tuple-element.587, s32[]{:T(128)} %constant.329.clone.1..sunk, s32[]{:T(128)} %constant.329.clone.1..sunk, s32[]{:T(128)} %constant.329.clone.1..sunk) | dynamic-update-slice | bytes 2621444 | tf_op jit(solution)/shard_map/while/body/jit(dynamic_update_index_in_dim)/dynamic_update_slice | solution.py:96
  490.9 7.7 reshape.665
  498.6 8.1 bitcast_add_fusion.3
  506.8 8.8 %copy.123 = f32[80,2,64,128]{0,1,3,2:T(2,128)} copy(f32[80,2,64,128]{3,2,1,0:T(8,128)} %bitcast_add_fusion.3) | data formatting | bytes 10485760 | tf_op jit(solution)/shard_map/add | solution.py:97
  524.5 7.7 reshape.666
  532.2 7.9 fusion.71
  543.8 10.1 %subtract_bitcast_fusion = f32[4,80,2,2048]{3,0,2,1:T(4,128)} fusion(f32[80,2,4,2048]{3,2,1,0:T(4,128)} %all_to_all.32, f32[2,4,2048]{2,1,0:T(4,128)S(1)} %div.148, f32[4,80,2,2048]{3,0,2,1:T(4,128)} %get-tuple-element.271), kind=kLoop, calls=%fused_computation.99 | loop fusion | flops 2621440 | bytes 15794176 | tf_op jit(solution)/shard_map/transpose | solution.py:80
  555.5 140.1 %while.25 = (s32[]{:T(128)}, f32[4,80,2,2048]{3,1,2,0:T(8,128)}, f32[4,80,2,2048]{3,0,2,1:T(4,128)}, f32[80,576]{1,0:T(8,128)S(1)}, s32[4]{0:T(128)S(1)}, /*inde...) while((s32[]{:T(128)}, f32[4,80,2,2048]{3,1,2,0:T(8,128)}, ...), condition=%wide.region_9.10_spmd, body=%wide.region_8.9_spmd.sunk | while | flops 4581785600 | bytes 33970356 | solution.py:96
  574.0 9.7 %fusion.121 = f32[2048,576]{0,1:T(8,128)S(1)} fusion(f32[576]{0:T(1024)S(1)} %reduce.31, f32[2048]{0:T(1024)S(1)} %get-tuple-element.571, f32[576]{0:T(1024)S(1)} %reduce.32, f32[2048]{0:T(1024)S(1)} %get-tuple-element.572), kind=kLoop, calls=%fused_computation.58.clone.1 | loop fusion | flops 49545216 | bytes 4739584 | tf_op jit(solution)/shard_map/while/body/eval_jaxpr/mul | solution.py:94
  587.6 7.9 fusion.119
  595.5 8.0 fusion.122
  604.8 9.7 %fusion.121 = f32[2048,576]{0,1:T(8,128)S(1)} fusion(f32[576]{0:T(1024)S(1)} %reduce.31, f32[2048]{0:T(1024)S(1)} %get-tuple-element.571, f32[576]{0:T(1024)S(1)} %reduce.32, f32[2048]{0:T(1024)S(1)} %get-tuple-element.572), kind=kLoop, calls=%fused_computation.58.clone.1 | loop fusion | flops 49545216 | bytes 4739584 | tf_op jit(solution)/shard_map/while/body/eval_jaxpr/mul | solution.py:94
  618.3 7.9 fusion.119
  626.2 7.9 fusion.122
  635.4 9.7 %fusion.121 = f32[2048,576]{0,1:T(8,128)S(1)} fusion(f32[576]{0:T(1024)S(1)} %reduce.31, f32[2048]{0:T(1024)S(1)} %get-tuple-element.571, f32[576]{0:T(1024)S(1)} %reduce.32, f32[2048]{0:T(1024)S(1)} %get-tuple-element.572), kind=kLoop, calls=%fused_computation.58.clone.1 | loop fusion | flops 49545216 | bytes 4739584 | tf_op jit(solution)/shard_map/while/body/eval_jaxpr/mul | solution.py:94
  649.0 7.9 fusion.119
  656.8 7.9 fusion.122
  666.0 9.7 %fusion.121 = f32[2048,576]{0,1:T(8,128)S(1)} fusion(f32[576]{0:T(1024)S(1)} %reduce.31, f32[2048]{0:T(1024)S(1)} %get-tuple-element.571, f32[576]{0:T(1024)S(1)} %reduce.32, f32[2048]{0:T(1024)S(1)} %get-tuple-element.572), kind=kLoop, calls=%fused_computation.58.clone.1 | loop fusion | flops 49545216 | bytes 4739584 | tf_op jit(solution)/shard_map/while/body/eval_jaxpr/mul | solution.py:94
  679.6 7.9 fusion.119
  687.5 7.9 fusion.122
  695.6 8.2 copy.131
  703.8 7.7 reshape.667
  716.8 119.1 %all_to_all.39 = f32[80,2,64,128]{3,2,1,0:T(8,128)S(1)} all-to-all(f32[80,2,64,128]{3,2,1,0:T(8,128)S(1)} %add.533), channel_id=1, replica_groups=mesh['lat'=4,'lon'=8] {'lon'}, dimensions={0} | all-to-all | bytes 10485760 | tf_op jit(solution)/shard_map/all_to_all | solution.py:98
  (135 shorter events, 96.8 us)
Async XLA Ops:
  27.5 6.5 copy-start.2
  27.5 6.6 copy-start.1
  27.5 6.7 copy-start
  27.5 7.1 copy-start.3
  27.5 123.1 %all-to-all-start = ((f32[8,1,163840]{2,1,0:T(1,128)}), f32[8,1,163840]{2,1,0:T(1,128)}, u32[]{:S(2)}, u32[]{:S(2)}) async-start(f32[8,1,163840]{2,1,0:T(1,128)} %reshape.700), calls=%async_computation | async-start | bytes 10485760 | tf_op jit(solution)/shard_map/all_to_all | solution.py:48
  193.1 13.8 %copy-start.4 = (f32[2,1,1,64]{3,2,1,0:T(1,128)S(1)}, f32[2,1,1,64]{3,2,1,0:T(1,128)}, u32[]{:S(2)}) copy-start(f32[2,1,1,64]{3,2,1,0:T(1,128)} %param.15) | copy-start | bytes 1540
  193.1 13.8 %copy-start.5 = (f32[2,1,1,64]{3,2,1,0:T(1,128)S(1)}, f32[2,1,1,64]{3,2,1,0:T(1,128)}, u32[]{:S(2)}) copy-start(f32[2,1,1,64]{3,2,1,0:T(1,128)} %param.14) | copy-start | bytes 1540
  207.9 23.6 %collective-permute-start = (f32[84,1,1,64]{0,3,2,1:T(8,128)S(1)}, f32[84,1,1,64]{0,3,2,1:T(8,128)S(1)}, u32[]{:S(2)}, u32[]{:S(2)}) collective-permute-start(f32[84,1,1,64]{0,3,2,1:T(8,128)S(1)} %bitcast.205), channel_id=1, source_target_pairs={{0,8},{8,16},{16,24},{24,0},{1,9},{9,17},{17,25},{25,1},{2,10},{10... | collective-permute-start | bytes 64520 | tf_op jit(solution)/shard_map/ppermute | solution.py:17
  209.5 22.1 %collective-permute-start.1 = (f32[84,1,1,64]{0,3,2,1:T(8,128)S(1)}, f32[84,1,1,64]{0,3,2,1:T(8,128)S(1)}, u32[]{:S(2)}, u32[]{:S(2)}) collective-permute-start(f32[84,1,1,64]{0,3,2,1:T(8,128)S(1)} %bitcast.206), channel_id=1, source_target_pairs={{8,0},{16,8},{24,16},{0,24},{9,1},{17,9},{25,17},{1,25},{10,2},{18... | collective-permute-start | bytes 64520 | tf_op jit(solution)/shard_map/ppermute | solution.py:20
  231.6 10.8 %collective-permute-start.2 = (f32[84,3,1,64]{0,3,2,1:T(8,128)S(1)}, f32[84,3,1,64]{0,3,2,1:T(8,128)S(1)}, u32[]{:S(2)}, u32[]{:S(2)}) collective-permute-start(f32[84,3,1,64]{0,3,2,1:T(8,128)S(1)} %pad_maximum_fusion.2), channel_id=1, source_target_pairs={{0,1},{1,2},{2,3},{3,4},{4,5},{5,6},{6,7},{7,0},{8,9},{9,10},{10,1... | collective-permute-start | bytes 193544 | tf_op jit(solution)/shard_map/ppermute | solution.py:17
  231.7 10.7 %collective-permute-start.3 = (f32[84,3,1,64]{0,3,2,1:T(8,128)S(1)}, f32[84,3,1,64]{0,3,2,1:T(8,128)S(1)}, u32[]{:S(2)}, u32[]{:S(2)}) collective-permute-start(f32[84,3,1,64]{0,3,2,1:T(8,128)S(1)} %pad_maximum_fusion.2), channel_id=1, source_target_pairs={{1,0},{2,1},{3,2},{4,3},{5,4},{6,5},{7,6},{0,7},{9,8},{10,9},{11,1... | collective-permute-start | bytes 193544 | tf_op jit(solution)/shard_map/ppermute | solution.py:20
  521.5 18.7 %collective-permute-start.4 = (f32[84,1,1,64]{0,3,2,1:T(8,128)S(1)}, f32[84,1,1,64]{0,3,2,1:T(8,128)S(1)}, u32[]{:S(2)}, u32[]{:S(2)}) collective-permute-start(f32[84,1,1,64]{0,3,2,1:T(8,128)S(1)} %bitcast.201), channel_id=1, source_target_pairs={{0,8},{8,16},{16,24},{24,0},{1,9},{9,17},{17,25},{25,1},{2,10},{10... | collective-permute-start | bytes 64520 | tf_op jit(solution)/shard_map/ppermute | solution.py:17
  522.2 18.0 %collective-permute-start.5 = (f32[84,1,1,64]{0,3,2,1:T(8,128)S(1)}, f32[84,1,1,64]{0,3,2,1:T(8,128)S(1)}, u32[]{:S(2)}, u32[]{:S(2)}) collective-permute-start(f32[84,1,1,64]{0,3,2,1:T(8,128)S(1)} %bitcast.202), channel_id=1, source_target_pairs={{8,0},{16,8},{24,16},{0,24},{9,1},{17,9},{25,17},{1,25},{10,2},{18... | collective-permute-start | bytes 64520 | tf_op jit(solution)/shard_map/ppermute | solution.py:20
  540.2 13.7 %collective-permute-start.6 = (f32[84,3,1,64]{0,3,2,1:T(8,128)S(1)}, f32[84,3,1,64]{0,3,2,1:T(8,128)S(1)}, u32[]{:S(2)}, u32[]{:S(2)}) collective-permute-start(f32[84,3,1,64]{0,3,2,1:T(8,128)S(1)} %pad_maximum_fusion.3), channel_id=1, source_target_pairs={{0,1},{1,2},{2,3},{3,4},{4,5},{5,6},{6,7},{7,0},{8,9},{9,10},{10,1... | collective-permute-start | bytes 193544 | tf_op jit(solution)/shard_map/ppermute | solution.py:17
  540.3 13.6 %collective-permute-start.7 = (f32[84,3,1,64]{0,3,2,1:T(8,128)S(1)}, f32[84,3,1,64]{0,3,2,1:T(8,128)S(1)}, u32[]{:S(2)}, u32[]{:S(2)}) collective-permute-start(f32[84,3,1,64]{0,3,2,1:T(8,128)S(1)} %pad_maximum_fusion.3), channel_id=1, source_target_pairs={{1,0},{2,1},{3,2},{4,3},{5,4},{6,5},{7,6},{0,7},{9,8},{10,9},{11,1... | collective-permute-start | bytes 193544 | tf_op jit(solution)/shard_map/ppermute | solution.py:20
where the time goes:
time: 852 us; the launch traced here: 839 us
  local copies, waits for them, and re-layouts  274 us (32%)
  other arithmetic  138 us (16%)
  matrix products  123 us (14%)
  blocking collectives  119 us (14%)
  waiting for transfers between devices  115 us (13%)
  loops' own time  49.7 us (6%)
  starting transfers between devices  19.8 us (2%)
    all_to_all x1, blocking collectives, body(): return lax.all_to_all(state, 'lon', split_axis=0, concat_axis=3, tiled=True)  119 us
    all_to_all x1, waiting for transfers between devices, body(): lax.all_to_all(members, 'lon', split_axis=3, concat_axis=0, tiled=True)  115 us
    dynamic_update_slice x8, local copies, waits for them, and re-layouts, body(): increments = lax.map(one_block, (blocks, jnp.arange(block_count)))  102 us
    mul x8, other arithmetic, one_block(): return jnp.einsum('pcm,mk->kpc', cov * taper[None], coef, precision=highest)  77.2 us
    dot_general x8, matrix products, one_block(): jnp.einsum('kpc,km->pcm', block, prior_pert, precision=highest)  62.8 us
    dot_general x8, matrix products, one_block(): return jnp.einsum('pcm,mk->kpc', cov * taper[None], coef, precision=highest)  58.8 us
    another operation x2, loops' own time, body(): increments = lax.map(one_block, (blocks, jnp.arange(block_count)))  49.7 us
    unnamed x15, local copies, waits for them, and re-layouts  40.7 us
  transfers between devices with their start and end apart: 9, of which 1 were waited for; matrix products, arithmetic and copies ran while one was open for 6% of the time, Pallas kernels for 0%

commit v1 on v0

--- a/solution.py
+++ b/solution.py
@@ -45,7 +45,10 @@
     lat_first = lax.axis_index("lat") * clat
     lon_first = lax.axis_index("lon") * clon
     highest = lax.Precision.HIGHEST
-    state = lax.all_to_all(members, "lon", split_axis=3, concat_axis=0, tiled=True)
+    state = jnp.concatenate(
+        lax.all_to_all(jnp.stack(jnp.split(members, lax.axis_size("lon"), axis=3)), "lon", 0, 0),
+        axis=0,
+    )
     first_left = 0
     for batch in range(first_left, NBATCH):
         picked = state[:, :, obs_row[batch, 0, 0], obs_col[batch, 0, 0]]

time: 852 us -> 755 us (0.89)
  local copies, waits for them, and re-layouts: 274 us -> 226 us
  loops' own time: 49.7 us -> 24.8 us
  other arithmetic: 138 us -> 118 us
    all_to_all x5 -> x0, local copies, waits for them, and re-layouts: 39.1 us -> none  [body(): lax.all_to_all(members, 'lon', split_axis=3, concat_axis=0, tiled=True)]
    unnamed x15 -> x19, local copies, waits for them, and re-layouts: 40.7 us -> 14 us
    another operation x2, loops' own time: 49.7 us -> 24.8 us  [body(): increments = lax.map(one_block, (blocks, jnp.arange(block_count)))]
    all_to_all x1 -> x0, other arithmetic: 16.6 us -> none  [body(): lax.all_to_all(members, 'lon', split_axis=3, concat_axis=0, tiled=True)]
    reshape x0 -> x2, local copies, waits for them, and re-layouts: none -> 16 us  [body(): jnp.concatenate(lax.all_to_all(jnp.stack(jnp.split(members, lax.axis_size...]
  transfers between devices with their start and end apart: 9 -> 9, of which waited for: 1 -> 1; matrix products, arithmetic and copies ran while one was open for 6% -> 5% of each run, Pallas kernels for 0% -> 0%
where the time goes in v1:
time: 755 us; the launch traced here: 747 us
  local copies, waits for them, and re-layouts  226 us (30%)
  matrix products  123 us (16%)
  blocking collectives  119 us (16%)
  other arithmetic  118 us (16%)
  waiting for transfers between devices  115 us (15%)
  loops' own time  24.8 us (3%)
  starting transfers between devices  19.6 us (3%)
    all_to_all x1, blocking collectives, body(): return lax.all_to_all(state, 'lon', split_axis=0, concat_axis=3, tiled=True)  119 us
    all_to_all x1, waiting for transfers between devices, body(): lax.all_to_all(jnp.stack(jnp.split(members, lax.axis_size('lon'), axis=3)...  115 us
    dynamic_update_slice x8, local copies, waits for them, and re-layouts, body(): increments = lax.map(one_block, (blocks, jnp.arange(block_count)))  102 us
    mul x8, other arithmetic, one_block(): return jnp.einsum('pcm,mk->kpc', cov * taper[None], coef, precision=highest)  77.2 us
    dot_general x8, matrix products, one_block(): jnp.einsum('kpc,km->pcm', block, prior_pert, precision=highest)  62.8 us
    dot_general x8, matrix products, one_block(): return jnp.einsum('pcm,mk->kpc', cov * taper[None], coef, precision=highest)  58.8 us
    dynamic_slice x16, local copies, waits for them, and re-layouts, body(): increments = lax.map(one_block, (blocks, jnp.arange(block_count)))  36.4 us
    another operation x2, loops' own time, body(): increments = lax.map(one_block, (blocks, jnp.arange(block_count)))  24.8 us
  transfers between devices with their start and end apart: 9, of which 1 were waited for; matrix products, arithmetic and copies ran while one was open for 5% of the time, Pallas kernels for 0%

profile of v1, /device:TPU:0, one launch (start us, length us, event | category | flops | bytes accessed | tf_op | source)
XLA Modules:
  0.0 746.7 jit_solution(16874692228037967735)
XLA Ops:
  16.0 6.5 all-to-all-start
  23.8 115.3 %all-to-all-done = f32[8,10,2,64,128]{4,3,2,1,0:T(8,128)} async-done(((f32[8,10,2,64,128]{4,3,2,1,0:T(8,128)}), f32[8,10,2,64,128]{4,3,2,1,0:T(8,128)}, u32[]{:S(2)}, u32[]{:S(2)}) %all-to-all-start) | async-done | bytes 5242912 | tf_op jit(solution)/shard_map/all_to_all | solution.py:49
  139.1 8.8 %copy.73 = f32[80,2,64,128]{0,1,3,2:T(2,128)} copy(f32[80,2,64,128]{3,2,1,0:T(8,128)} %bitcast.20) | data formatting | bytes 10485760 | tf_op jit(solution)/shard_map/reshape | solution.py:48
  147.9 4.1 gather_fusion
  159.7 7.2 reshape.671
  170.5 7.2 subtract_bitcast_fusion.1
  179.3 238.8 %while.24 = (s32[]{:T(128)}, f32[4,80,2,2048]{3,0,2,1:T(4,128)}, f32[4,80,2,2048]{3,0,2,1:T(4,128)}, f32[80,576]{1,0:T(8,128)S(1)}, s32[4]{0:T(128)S(1)}, /*inde...) while((s32[]{:T(128)}, f32[4,80,2,2048]{3,0,2,1:T(4,128)}, ...), condition=%wide.region_4.5_spmd, body=%wide.region_3.4_spmd.sunk | while | flops 4581785600 | bytes 39212736 | solution.py:99
  199.0 9.7 %fusion.113 = f32[2048,576]{0,1:T(8,128)S(1)} fusion(f32[576]{0:T(1024)S(1)} %reduce.28, f32[2048]{0:T(1024)S(1)} %get-tuple-element.539, f32[576]{0:T(1024)S(1)} %reduce.29, f32[2048]{0:T(1024)S(1)} %get-tuple-element.540), kind=kLoop, calls=%fused_computation.12.clone.1 | loop fusion | flops 49545216 | bytes 4739584 | tf_op jit(solution)/shard_map/while/body/eval_jaxpr/mul | solution.py:97
  208.6 3.9 constant_dynamic-slice_fusion.4
  212.6 7.8 %fusion.111 = f32[2,2048,576]{1,2,0:T(8,128)S(1)} fusion(f32[1,80,2,2048]{3,0,2,1:T(1,128)S(1)} %constant_dynamic-slice_fusion.4, f32[80,576]{1,0:T(8,128)S(1)} %get-tuple-element.584), kind=kOutput, calls=%fused_computation.29.clone.1 | convolution fusion | flops 2264924160 | bytes 10932224 | tf_op jit(solution)/shard_map/while/body/eval_jaxpr/kpc,km->pcm/dot_general | solution.py:94
  220.4 6.8 fusion.114
  228.6 24.1 %dynamic_update_slice.16 = f32[4,80,2,2048]{3,0,2,1:T(4,128)} dynamic-update-slice(f32[4,80,2,2048]{3,0,2,1:T(4,128)} %get-tuple-element.568, f32[1,80,2,2048]{3,0,2,1:T(1,128)S(1)} %copy.117, s32[]{:T(128)} %get-tuple-element.567, s32[]{:T(128)} %constant.329.clone.1..sunk, s32[]{:T(128)} %constant.329.clone.1..sunk, s32[]{:T(128)} %constant.329.clone.1..sunk) | dynamic-update-slice | bytes 2621444 | tf_op jit(solution)/shard_map/while/body/jit(dynamic_update_index_in_dim)/dynamic_update_slice | solution.py:99
  254.0 9.7 %fusion.113 = f32[2048,576]{0,1:T(8,128)S(1)} fusion(f32[576]{0:T(1024)S(1)} %reduce.28, f32[2048]{0:T(1024)S(1)} %get-tuple-element.539, f32[576]{0:T(1024)S(1)} %reduce.29, f32[2048]{0:T(1024)S(1)} %get-tuple-element.540), kind=kLoop, calls=%fused_computation.12.clone.1 | loop fusion | flops 49545216 | bytes 4739584 | tf_op jit(solution)/shard_map/while/body/eval_jaxpr/mul | solution.py:97
  267.6 7.8 %fusion.111 = f32[2,2048,576]{1,2,0:T(8,128)S(1)} fusion(f32[1,80,2,2048]{3,0,2,1:T(1,128)S(1)} %constant_dynamic-slice_fusion.4, f32[80,576]{1,0:T(8,128)S(1)} %get-tuple-element.584), kind=kOutput, calls=%fused_computation.29.clone.1 | convolution fusion | flops 2264924160 | bytes 10932224 | tf_op jit(solution)/shard_map/while/body/eval_jaxpr/kpc,km->pcm/dot_general | solution.py:94
  275.4 6.8 fusion.114
  283.6 24.1 %dynamic_update_slice.16 = f32[4,80,2,2048]{3,0,2,1:T(4,128)} dynamic-update-slice(f32[4,80,2,2048]{3,0,2,1:T(4,128)} %get-tuple-element.568, f32[1,80,2,2048]{3,0,2,1:T(1,128)S(1)} %copy.117, s32[]{:T(128)} %get-tuple-element.567, s32[]{:T(128)} %constant.329.clone.1..sunk, s32[]{:T(128)} %constant.329.clone.1..sunk, s32[]{:T(128)} %constant.329.clone.1..sunk) | dynamic-update-slice | bytes 2621444 | tf_op jit(solution)/shard_map/while/body/jit(dynamic_update_index_in_dim)/dynamic_update_slice | solution.py:99
  309.0 9.7 %fusion.113 = f32[2048,576]{0,1:T(8,128)S(1)} fusion(f32[576]{0:T(1024)S(1)} %reduce.28, f32[2048]{0:T(1024)S(1)} %get-tuple-element.539, f32[576]{0:T(1024)S(1)} %reduce.29, f32[2048]{0:T(1024)S(1)} %get-tuple-element.540), kind=kLoop, calls=%fused_computation.12.clone.1 | loop fusion | flops 49545216 | bytes 4739584 | tf_op jit(solution)/shard_map/while/body/eval_jaxpr/mul | solution.py:97
  322.6 7.8 %fusion.111 = f32[2,2048,576]{1,2,0:T(8,128)S(1)} fusion(f32[1,80,2,2048]{3,0,2,1:T(1,128)S(1)} %constant_dynamic-slice_fusion.4, f32[80,576]{1,0:T(8,128)S(1)} %get-tuple-element.584), kind=kOutput, calls=%fused_computation.29.clone.1 | convolution fusion | flops 2264924160 | bytes 10932224 | tf_op jit(solution)/shard_map/while/body/eval_jaxpr/kpc,km->pcm/dot_general | solution.py:94
  330.5 6.8 fusion.114
  338.6 24.1 %dynamic_update_slice.16 = f32[4,80,2,2048]{3,0,2,1:T(4,128)} dynamic-update-slice(f32[4,80,2,2048]{3,0,2,1:T(4,128)} %get-tuple-element.568, f32[1,80,2,2048]{3,0,2,1:T(1,128)S(1)} %copy.117, s32[]{:T(128)} %get-tuple-element.567, s32[]{:T(128)} %constant.329.clone.1..sunk, s32[]{:T(128)} %constant.329.clone.1..sunk, s32[]{:T(128)} %constant.329.clone.1..sunk) | dynamic-update-slice | bytes 2621444 | tf_op jit(solution)/shard_map/while/body/jit(dynamic_update_index_in_dim)/dynamic_update_slice | solution.py:99
  364.0 9.7 %fusion.113 = f32[2048,576]{0,1:T(8,128)S(1)} fusion(f32[576]{0:T(1024)S(1)} %reduce.28, f32[2048]{0:T(1024)S(1)} %get-tuple-element.539, f32[576]{0:T(1024)S(1)} %reduce.29, f32[2048]{0:T(1024)S(1)} %get-tuple-element.540), kind=kLoop, calls=%fused_computation.12.clone.1 | loop fusion | flops 49545216 | bytes 4739584 | tf_op jit(solution)/shard_map/while/body/eval_jaxpr/mul | solution.py:97
  377.6 7.8 %fusion.111 = f32[2,2048,576]{1,2,0:T(8,128)S(1)} fusion(f32[1,80,2,2048]{3,0,2,1:T(1,128)S(1)} %constant_dynamic-slice_fusion.4, f32[80,576]{1,0:T(8,128)S(1)} %get-tuple-element.584), kind=kOutput, calls=%fused_computation.29.clone.1 | convolution fusion | flops 2264924160 | bytes 10932224 | tf_op jit(solution)/shard_map/while/body/eval_jaxpr/kpc,km->pcm/dot_general | solution.py:94
  385.5 6.8 fusion.114
  393.6 24.1 %dynamic_update_slice.16 = f32[4,80,2,2048]{3,0,2,1:T(4,128)} dynamic-update-slice(f32[4,80,2,2048]{3,0,2,1:T(4,128)} %get-tuple-element.568, f32[1,80,2,2048]{3,0,2,1:T(1,128)S(1)} %copy.117, s32[]{:T(128)} %get-tuple-element.567, s32[]{:T(128)} %constant.329.clone.1..sunk, s32[]{:T(128)} %constant.329.clone.1..sunk, s32[]{:T(128)} %constant.329.clone.1..sunk) | dynamic-update-slice | bytes 2621444 | tf_op jit(solution)/shard_map/while/body/jit(dynamic_update_index_in_dim)/dynamic_update_slice | solution.py:99
  418.2 7.7 %reshape.672 = f32[80,2,64,128]{3,2,1,0:T(8,128)} reshape(f32[80,2,4,2048]{3,2,1,0:T(4,128)} %bitcast.194) | data formatting | bytes 10485760 | tf_op jit(solution)/shard_map/reshape | solution.py:100
  425.8 8.1 %bitcast_add_fusion.2 = f32[80,2,64,128]{3,2,1,0:T(8,128)} fusion(f32[80,2,64,128]{3,2,1,0:T(8,128)} %reshape.672, f32[8,10,2,64,128]{4,3,2,1,0:T(8,128)} %all-to-all-done), kind=kLoop, calls=%fused_computation.169 | loop fusion | flops 1310720 | bytes 15728640 | tf_op jit(solution)/shard_map/add | solution.py:100
  434.0 8.8 %copy.82 = f32[80,2,64,128]{0,1,3,2:T(2,128)} copy(f32[80,2,64,128]{3,2,1,0:T(8,128)} %bitcast_add_fusion.2) | data formatting | bytes 10485760 | tf_op jit(solution)/shard_map/add | solution.py:100
  442.8 4.1 gather_fusion.1
  451.7 7.7 %reshape.673 = f32[8,10,2,64,128]{4,3,2,1,0:T(8,128)} reshape(f32[80,2,4,2048]{3,2,1,0:T(4,128)} %bitcast.195) | data formatting | bytes 10485760 | tf_op jit(solution)/shard_map/reshape | solution.py:100
  459.4 4.7 add_reduce_fusion
  467.8 10.1 %subtract_bitcast_fusion = f32[4,80,2,2048]{3,0,2,1:T(4,128)} fusion(f32[80,2,4,2048]{3,2,1,0:T(4,128)} %reshape.671, f32[2,4,2048]{2,1,0:T(4,128)S(1)} %div.148, f32[4,80,2,2048]{3,0,2,1:T(4,128)} %get-tuple-element.271), kind=kLoop, calls=%fused_computation.96 | loop fusion | flops 2621440 | bytes 15794176 | tf_op jit(solution)/shard_map/transpose | solution.py:83
  479.5 123.5 %while.25 = (s32[]{:T(128)}, f32[4,80,2,2048]{3,1,2,0:T(8,128)}, f32[4,80,2,2048]{3,0,2,1:T(4,128)}, f32[80,576]{1,0:T(8,128)S(1)}, s32[4]{0:T(128)S(1)}, /*inde...) while((s32[]{:T(128)}, f32[4,80,2,2048]{3,1,2,0:T(8,128)}, ...), condition=%wide.region_9.10_spmd, body=%wide.region_8.9_spmd.sunk | while | flops 4581785600 | bytes 33970356 | solution.py:99
  481.0 9.7 %fusion.120 = f32[2048,576]{0,1:T(8,128)S(1)} fusion(f32[576]{0:T(1024)S(1)} %reduce.30, f32[2048]{0:T(1024)S(1)} %get-tuple-element.551, f32[576]{0:T(1024)S(1)} %reduce.31, f32[2048]{0:T(1024)S(1)} %get-tuple-element.552), kind=kLoop, calls=%fused_computation.58.clone.1 | loop fusion | flops 49545216 | bytes 4739584 | tf_op jit(solution)/shard_map/while/body/eval_jaxpr/mul | solution.py:97
  494.6 7.9 %fusion.118 = f32[2,2048,576]{1,2,0:T(8,128)S(1)} fusion(f32[1,80,2,2048]{3,0,2,1:T(1,128)S(1)} %constant_dynamic-slice_fusion.5, f32[80,576]{1,0:T(8,128)S(1)} %get-tuple-element.624), kind=kOutput, calls=%fused_computation.76.clone.1 | convolution fusion | flops 2264924160 | bytes 10932224 | tf_op jit(solution)/shard_map/while/body/eval_jaxpr/kpc,km->pcm/dot_general | solution.py:94
  502.5 8.0 %fusion.121 = f32[4,80,2,2048]{3,1,2,0:T(8,128)} fusion(f32[4,80,2,2048]{3,1,2,0:T(8,128)} %get-tuple-element.609, s32[]{:T(128)} %get-tuple-element.608, f32[2,2048,576]{1,2,0:T(8,128)S(1)} %fusion.118, f32[2048,576]{0,1:T(8,128)S(1)} %fusion.120, f32[576,80]{0,1:T(8,128)S(1)} %get-tuple-element.630), kind=kOutput, calls=%fused_computation.74.clone.1 | convolution fusion | flops 2267283456 | bytes 15651328 | tf_op jit(solution)/shard_map/while/body/eval_jaxpr/pcm,mk->kpc/dot_general | solution.py:97
  511.9 9.7 %fusion.120 = f32[2048,576]{0,1:T(8,128)S(1)} fusion(f32[576]{0:T(1024)S(1)} %reduce.30, f32[2048]{0:T(1024)S(1)} %get-tuple-element.551, f32[576]{0:T(1024)S(1)} %reduce.31, f32[2048]{0:T(1024)S(1)} %get-tuple-element.552), kind=kLoop, calls=%fused_computation.58.clone.1 | loop fusion | flops 49545216 | bytes 4739584 | tf_op jit(solution)/shard_map/while/body/eval_jaxpr/mul | solution.py:97
  525.4 7.9 %fusion.118 = f32[2,2048,576]{1,2,0:T(8,128)S(1)} fusion(f32[1,80,2,2048]{3,0,2,1:T(1,128)S(1)} %constant_dynamic-slice_fusion.5, f32[80,576]{1,0:T(8,128)S(1)} %get-tuple-element.624), kind=kOutput, calls=%fused_computation.76.clone.1 | convolution fusion | flops 2264924160 | bytes 10932224 | tf_op jit(solution)/shard_map/while/body/eval_jaxpr/kpc,km->pcm/dot_general | solution.py:94
  533.3 7.9 %fusion.121 = f32[4,80,2,2048]{3,1,2,0:T(8,128)} fusion(f32[4,80,2,2048]{3,1,2,0:T(8,128)} %get-tuple-element.609, s32[]{:T(128)} %get-tuple-element.608, f32[2,2048,576]{1,2,0:T(8,128)S(1)} %fusion.118, f32[2048,576]{0,1:T(8,128)S(1)} %fusion.120, f32[576,80]{0,1:T(8,128)S(1)} %get-tuple-element.630), kind=kOutput, calls=%fused_computation.74.clone.1 | convolution fusion | flops 2267283456 | bytes 15651328 | tf_op jit(solution)/shard_map/while/body/eval_jaxpr/pcm,mk->kpc/dot_general | solution.py:97
  542.6 9.7 %fusion.120 = f32[2048,576]{0,1:T(8,128)S(1)} fusion(f32[576]{0:T(1024)S(1)} %reduce.30, f32[2048]{0:T(1024)S(1)} %get-tuple-element.551, f32[576]{0:T(1024)S(1)} %reduce.31, f32[2048]{0:T(1024)S(1)} %get-tuple-element.552), kind=kLoop, calls=%fused_computation.58.clone.1 | loop fusion | flops 49545216 | bytes 4739584 | tf_op jit(solution)/shard_map/while/body/eval_jaxpr/mul | solution.py:97
  556.2 7.9 %fusion.118 = f32[2,2048,576]{1,2,0:T(8,128)S(1)} fusion(f32[1,80,2,2048]{3,0,2,1:T(1,128)S(1)} %constant_dynamic-slice_fusion.5, f32[80,576]{1,0:T(8,128)S(1)} %get-tuple-element.624), kind=kOutput, calls=%fused_computation.76.clone.1 | convolution fusion | flops 2264924160 | bytes 10932224 | tf_op jit(solution)/shard_map/while/body/eval_jaxpr/kpc,km->pcm/dot_general | solution.py:94
  564.1 7.9 %fusion.121 = f32[4,80,2,2048]{3,1,2,0:T(8,128)} fusion(f32[4,80,2,2048]{3,1,2,0:T(8,128)} %get-tuple-element.609, s32[]{:T(128)} %get-tuple-element.608, f32[2,2048,576]{1,2,0:T(8,128)S(1)} %fusion.118, f32[2048,576]{0,1:T(8,128)S(1)} %fusion.120, f32[576,80]{0,1:T(8,128)S(1)} %get-tuple-element.630), kind=kOutput, calls=%fused_computation.74.clone.1 | convolution fusion | flops 2267283456 | bytes 15651328 | tf_op jit(solution)/shard_map/while/body/eval_jaxpr/pcm,mk->kpc/dot_general | solution.py:97
  573.3 9.7 %fusion.120 = f32[2048,576]{0,1:T(8,128)S(1)} fusion(f32[576]{0:T(1024)S(1)} %reduce.30, f32[2048]{0:T(1024)S(1)} %get-tuple-element.551, f32[576]{0:T(1024)S(1)} %reduce.31, f32[2048]{0:T(1024)S(1)} %get-tuple-element.552), kind=kLoop, calls=%fused_computation.58.clone.1 | loop fusion | flops 49545216 | bytes 4739584 | tf_op jit(solution)/shard_map/while/body/eval_jaxpr/mul | solution.py:97
  586.9 7.9 %fusion.118 = f32[2,2048,576]{1,2,0:T(8,128)S(1)} fusion(f32[1,80,2,2048]{3,0,2,1:T(1,128)S(1)} %constant_dynamic-slice_fusion.5, f32[80,576]{1,0:T(8,128)S(1)} %get-tuple-element.624), kind=kOutput, calls=%fused_computation.76.clone.1 | convolution fusion | flops 2264924160 | bytes 10932224 | tf_op jit(solution)/shard_map/while/body/eval_jaxpr/kpc,km->pcm/dot_general | solution.py:94
  594.8 7.9 %fusion.121 = f32[4,80,2,2048]{3,1,2,0:T(8,128)} fusion(f32[4,80,2,2048]{3,1,2,0:T(8,128)} %get-tuple-element.609, s32[]{:T(128)} %get-tuple-element.608, f32[2,2048,576]{1,2,0:T(8,128)S(1)} %fusion.118, f32[2048,576]{0,1:T(8,128)S(1)} %fusion.120, f32[576,80]{0,1:T(8,128)S(1)} %get-tuple-element.630), kind=kOutput, calls=%fused_computation.74.clone.1 | convolution fusion | flops 2267283456 | bytes 15651328 | tf_op jit(solution)/shard_map/while/body/eval_jaxpr/pcm,mk->kpc/dot_general | solution.py:97
  602.9 8.2 %copy.90 = f32[80,2,4,2048]{3,2,1,0:T(4,128)} copy(f32[80,2,4,2048]{3,0,1,2:T(8,128)} %bitcast.62) | data formatting | bytes 10485760 | tf_op jit(solution)/shard_map/transpose | solution.py:100
  611.1 7.7 %reshape.674 = f32[80,2,64,128]{3,2,1,0:T(8,128)} reshape(f32[80,2,4,2048]{3,2,1,0:T(4,128)} %copy.90) | data formatting | bytes 10485760 | tf_op jit(solution)/shard_map/reshape | solution.py:100
  618.8 5.3 add.533
  624.1 119.1 %all_to_all.23 = f32[80,2,64,128]{3,2,1,0:T(8,128)S(1)} all-to-all(f32[80,2,64,128]{3,2,1,0:T(8,128)S(1)} %add.533), channel_id=1, replica_groups=mesh['lat'=4,'lon'=8] {'lon'}, dimensions={0} | all-to-all | bytes 10485760 | tf_op jit(solution)/shard_map/all_to_all | solution.py:101
  (136 shorter events, 81.4 us)
Async XLA Ops:
  16.0 6.5 copy-start.2
  16.0 6.6 copy-start.1
  16.0 6.7 copy-start
  16.0 7.1 copy-start.3
  16.0 123.1 %all-to-all-start = ((f32[8,10,2,64,128]{4,3,2,1,0:T(8,128)}), f32[8,10,2,64,128]{4,3,2,1,0:T(8,128)}, u32[]{:S(2)}, u32[]{:S(2)}) async-start(f32[8,10,2,64,128]{4,3,2,1,0:T(8,128)} %bitcast_dynamic-update-slice_fusion), calls=%async_computation | async-start | bytes 10485760 | tf_op jit(solution)/shard_map/all_to_all | solution.py:49
  139.0 13.8 %copy-start.4 = (f32[2,1,1,64]{3,2,1,0:T(1,128)S(1)}, f32[2,1,1,64]{3,2,1,0:T(1,128)}, u32[]{:S(2)}) copy-start(f32[2,1,1,64]{3,2,1,0:T(1,128)} %param.15) | copy-start | bytes 1540
  139.1 13.8 %copy-start.5 = (f32[2,1,1,64]{3,2,1,0:T(1,128)S(1)}, f32[2,1,1,64]{3,2,1,0:T(1,128)}, u32[]{:S(2)}) copy-start(f32[2,1,1,64]{3,2,1,0:T(1,128)} %param.14) | copy-start | bytes 1540
  153.9 13.0 %collective-permute-start = (f32[84,1,1,64]{0,3,2,1:T(8,128)S(1)}, f32[84,1,1,64]{0,3,2,1:T(8,128)S(1)}, u32[]{:S(2)}, u32[]{:S(2)}) collective-permute-start(f32[84,1,1,64]{0,3,2,1:T(8,128)S(1)} %bitcast.205), channel_id=1, source_target_pairs={{0,8},{8,16},{16,24},{24,0},{1,9},{9,17},{17,25},{25,1},{2,10},{10... | collective-permute-start | bytes 64520 | tf_op jit(solution)/shard_map/ppermute | solution.py:17
  155.4 11.5 %collective-permute-start.1 = (f32[84,1,1,64]{0,3,2,1:T(8,128)S(1)}, f32[84,1,1,64]{0,3,2,1:T(8,128)S(1)}, u32[]{:S(2)}, u32[]{:S(2)}) collective-permute-start(f32[84,1,1,64]{0,3,2,1:T(8,128)S(1)} %bitcast.206), channel_id=1, source_target_pairs={{8,0},{16,8},{24,16},{0,24},{9,1},{17,9},{25,17},{1,25},{10,2},{18... | collective-permute-start | bytes 64520 | tf_op jit(solution)/shard_map/ppermute | solution.py:20
  166.9 10.8 %collective-permute-start.2 = (f32[84,3,1,64]{0,3,2,1:T(8,128)S(1)}, f32[84,3,1,64]{0,3,2,1:T(8,128)S(1)}, u32[]{:S(2)}, u32[]{:S(2)}) collective-permute-start(f32[84,3,1,64]{0,3,2,1:T(8,128)S(1)} %pad_maximum_fusion.2), channel_id=1, source_target_pairs={{0,1},{1,2},{2,3},{3,4},{4,5},{5,6},{6,7},{7,0},{8,9},{9,10},{10,1... | collective-permute-start | bytes 193544 | tf_op jit(solution)/shard_map/ppermute | solution.py:17
  167.0 10.7 %collective-permute-start.3 = (f32[84,3,1,64]{0,3,2,1:T(8,128)S(1)}, f32[84,3,1,64]{0,3,2,1:T(8,128)S(1)}, u32[]{:S(2)}, u32[]{:S(2)}) collective-permute-start(f32[84,3,1,64]{0,3,2,1:T(8,128)S(1)} %pad_maximum_fusion.2), channel_id=1, source_target_pairs={{1,0},{2,1},{3,2},{4,3},{5,4},{6,5},{7,6},{0,7},{9,8},{10,9},{11,1... | collective-permute-start | bytes 193544 | tf_op jit(solution)/shard_map/ppermute | solution.py:20
  448.7 15.4 %collective-permute-start.4 = (f32[84,1,1,64]{0,3,2,1:T(8,128)S(1)}, f32[84,1,1,64]{0,3,2,1:T(8,128)S(1)}, u32[]{:S(2)}, u32[]{:S(2)}) collective-permute-start(f32[84,1,1,64]{0,3,2,1:T(8,128)S(1)} %bitcast.201), channel_id=1, source_target_pairs={{0,8},{8,16},{16,24},{24,0},{1,9},{9,17},{17,25},{25,1},{2,10},{10... | collective-permute-start | bytes 64520 | tf_op jit(solution)/shard_map/ppermute | solution.py:17
  449.4 14.8 %collective-permute-start.5 = (f32[84,1,1,64]{0,3,2,1:T(8,128)S(1)}, f32[84,1,1,64]{0,3,2,1:T(8,128)S(1)}, u32[]{:S(2)}, u32[]{:S(2)}) collective-permute-start(f32[84,1,1,64]{0,3,2,1:T(8,128)S(1)} %bitcast.202), channel_id=1, source_target_pairs={{8,0},{16,8},{24,16},{0,24},{9,1},{17,9},{25,17},{1,25},{10,2},{18... | collective-permute-start | bytes 64520 | tf_op jit(solution)/shard_map/ppermute | solution.py:20
  464.2 13.7 %collective-permute-start.6 = (f32[84,3,1,64]{0,3,2,1:T(8,128)S(1)}, f32[84,3,1,64]{0,3,2,1:T(8,128)S(1)}, u32[]{:S(2)}, u32[]{:S(2)}) collective-permute-start(f32[84,3,1,64]{0,3,2,1:T(8,128)S(1)} %pad_maximum_fusion.3), channel_id=1, source_target_pairs={{0,1},{1,2},{2,3},{3,4},{4,5},{5,6},{6,7},{7,0},{8,9},{9,10},{10,1... | collective-permute-start | bytes 193544 | tf_op jit(solution)/shard_map/ppermute | solution.py:17
  464.2 13.6 %collective-permute-start.7 = (f32[84,3,1,64]{0,3,2,1:T(8,128)S(1)}, f32[84,3,1,64]{0,3,2,1:T(8,128)S(1)}, u32[]{:S(2)}, u32[]{:S(2)}) collective-permute-start(f32[84,3,1,64]{0,3,2,1:T(8,128)S(1)} %pad_maximum_fusion.3), channel_id=1, source_target_pairs={{1,0},{2,1},{3,2},{4,3},{5,4},{6,5},{7,6},{0,7},{9,8},{10,9},{11,1... | collective-permute-start | bytes 193544 | tf_op jit(solution)/shard_map/ppermute | solution.py:20
